TPU v7x, 32 devices: a whole 2x2x4 slice. The times are simulated.
32 devices in a mesh: tile: 8 (over z, y), date: 4 (over x, core).
Axes of the slice: x: 2, y: 2, z: 4, core: 2. Of those that a mesh axis runs over, the one named last changes fastest.
Arguments:
- complex_images: bfloat16 [8, 8, 8, 2, 10, 1920], P('date', 'tile')
- segment_position_map: int32 [8, 8], P('tile'), may hold values from 0 to 7, each once within a row
- usable_position_total: int32 [8], P('tile'), may hold values from 4 to 8
- interferogram_epochs: int32 [16, 2], replicated, may hold values from 0 to 7, as said below
Outputs:
- coherence: float32 [16, 2, 16, 1024], P('date', None, None, 'tile')
Inputs may be any that keep to these rules, and one draw needn't show every extreme that they name: Each row of segment_position_map names every block position once. `interferogram_epochs`: the two dates of a pair differ.
All inputs are finite; a program needn't handle non-finite values.
Results may differ from a plain program's by a relative error of at most 0.0003.
Values may be sent and summed in bfloat16 or wider, within the bound.
A program may use at most 128 MiB of HBM per device.

v0:
```python
import jax
import jax.numpy as jnp
from jax import lax
from jax.sharding import PartitionSpec as P

LOOK_RG = 15
LOOK_AZ = 5


EPS = 1e-05


def tile_looks(stack, first_idx, second_idx, valid, box):
    scale = 1.0 / (LOOK_AZ * LOOK_RG)

    def looks(values):
        ranged = jnp.dot(
            values, box, precision=lax.Precision.HIGHEST, preferred_element_type=jnp.float32
        )
        extent = ranged.shape
        return (
            ranged.reshape(extent[:-2] + (extent[-2] // LOOK_AZ, LOOK_AZ, extent[-1])).sum(axis=-2)
            * scale
        )

    def date_power(image):
        image = image.astype(jnp.float32)
        return looks(image[:, 0] * image[:, 0] + image[:, 1] * image[:, 1])

    power = lax.map(date_power, stack)

    def one_pair(indices):
        first = lax.dynamic_index_in_dim(stack, indices[0], 0, keepdims=False).astype(jnp.float32)
        second = lax.dynamic_index_in_dim(stack, indices[1], 0, keepdims=False).astype(jnp.float32)
        cross_re = looks(first[:, 0] * second[:, 0] + first[:, 1] * second[:, 1])
        cross_im = looks(first[:, 1] * second[:, 0] - first[:, 0] * second[:, 1])
        power_first = lax.dynamic_index_in_dim(power, indices[0], 0, keepdims=False)
        power_second = lax.dynamic_index_in_dim(power, indices[1], 0, keepdims=False)
        weight = valid[:, None, None] / jnp.sqrt((power_first + EPS) * (power_second + EPS))
        return jnp.stack([cross_re * weight, cross_im * weight], axis=0)

    return lax.map(one_pair, jnp.stack([first_idx, second_idx], axis=1))


def place_rows(gamma, positions):
    ranking = jnp.argsort(positions)
    placed = jnp.take(gamma, ranking, axis=2)
    extent = placed.shape
    return placed.reshape(extent[0], extent[1], extent[2] * extent[3], extent[4])


def on_device(complex_images, segment_position_map, usable_position_total, interferogram_epochs):
    groups = lax.axis_size("date")
    tile_cols = complex_images.shape[-1]
    box = (
        jnp.arange(tile_cols)[:, None] // LOOK_RG == jnp.arange(tile_cols // LOOK_RG)[None, :]
    ).astype(jnp.float32)
    positions = segment_position_map[0]
    moved = lax.all_to_all(complex_images, "tile", split_axis=2, concat_axis=1, tiled=True)
    stack = moved[:, :, 0]
    valid = (positions < usable_position_total[0]).astype(jnp.float32)
    gathered = lax.all_gather(stack, "date", axis=0, tiled=True)
    mine = interferogram_epochs.shape[0] // groups
    local_pairs = lax.dynamic_slice_in_dim(
        interferogram_epochs, lax.axis_index("date") * mine, mine, 0
    )
    gamma = tile_looks(gathered, local_pairs[:, 0], local_pairs[:, 1], valid, box)
    return place_rows(gamma, positions)


def solution(mesh):
    in_specs = (P("date", "tile", None, None, None, None), P("tile", None), P("tile"), P())
    out_specs = P("date", None, None, "tile")
    return jax.shard_map(
        on_device, mesh=mesh, in_specs=in_specs, out_specs=out_specs, check_vma=False
    )
```

profile of v0, /device:TPU:0, one launch (start us, length us, event | category | flops | bytes accessed | tf_op | source)
XLA Modules:
  0.0 142.8 jit_solution(7151218420765707386)
XLA Ops:
  6.5 2.1 %copy.19 = bf16[2,1,8,2,10,1920]{5,3,4,1,0,2:T(2,128)(2,1)S(1)} copy(bf16[2,1,8,2,10,1920]{5,3,4,2,1,0:T(2,128)(2,1)} %param.8) | data formatting | bytes 2457600 | tf_op args[0]
  8.7 36.9 %all_to_all.4 = bf16[2,1,8,2,10,1920]{5,3,4,1,0,2:T(2,128)(2,1)S(1)} all-to-all(bf16[2,1,8,2,10,1920]{5,3,4,1,0,2:T(2,128)(2,1)S(1)} %copy.19), channel_id=1, replica_groups=mesh['tile'=8,'date'=4] {'tile'}, dimensions={2} | all-to-all | bytes 2457600 | tf_op jit(solution)/shard_map/all_to_all | solution.py:59
  45.6 1.2 copy.20
  47.5 1.0 sort.17
  48.7 35.6 %all-gather.3.cloned.1.call-done = bf16[8,1,8,2,10,1920]{5,2,4,3,1,0:T(8,128)(2,1)} async-done(((bf16[2,1,8,2,10,1920]{5,2,4,3,1,0:T(8,128)(2,1)}), bf16[8,1,8,2,10,1920]{5,2,4,3,1,0:T(8,128)(2,1)}) %all-gather.3.cloned.1.call-update) | async-done | bytes 4915216 | tf_op jit(solution)/shard_map/all_gather | solution.py:62
  84.4 17.9 %while.23 = (s32[]{:T(128)}, f32[8,8,2,128]{3,1,2,0:T(8,128)S(1)}, bf16[8,8,2,10,1920]{4,1,3,2,0:T(8,128)(2,1)}, s32[1920]{0:T(1024)S(1)}, s32[]{:T(128)}) while((s32[]{:T(128)}, f32[8,8,2,128]{3,1,2,0:T(8,128)S(1)}, bf16[8,8,2,10,1920]{4,1,3,2,0:T(8,128)(2,1)}, s32[1920]{0:T(1024)S(1)}, s32[]{:T(128)}) %tuple.60), condition=%wide.region_3.4_spmd.clone, body=%wide.region_1.3_spmd.clone.sunk | while | flops 237199360 | bytes 4333125 | solution.py:30
  84.4 1.2 bitcast_convert_fusion.5
  85.6 1.0 convolution_reduce_fusion.6
  86.6 1.2 bitcast_convert_fusion.5
  87.8 1.0 convolution_reduce_fusion.6
  88.8 1.2 bitcast_convert_fusion.5
  90.1 1.0 convolution_reduce_fusion.6
  91.1 1.2 bitcast_convert_fusion.5
  92.3 1.0 convolution_reduce_fusion.6
  93.3 1.2 bitcast_convert_fusion.5
  94.5 1.0 convolution_reduce_fusion.6
  95.5 1.2 bitcast_convert_fusion.5
  97.8 1.2 bitcast_convert_fusion.5
  100.0 1.2 bitcast_convert_fusion.5
  102.2 32.4 %while.24 = (s32[]{:T(128)}, f32[4,2,8,2,128]{4,0,3,2,1:T(4,128)S(1)}, s32[4,2]{0,1:T(2,128)S(1)}, bf16[8,8,2,10,1920]{4,1,3,2,0:T(8,128)(2,1)}, f32[8]{0:T(128)...) while((s32[]{:T(128)}, ...), condition=%wide.region_7.8_spmd.clone.clone, body=%wide.region_4.7_spmd.clone.clone.sunk | while | flops 474415104 | bytes 8781057 | solution.py:42
  106.6 1.4 bitcast_convert_fusion.6
  114.7 1.4 bitcast_convert_fusion.6
  122.8 1.4 bitcast_convert_fusion.6
  130.9 1.4 bitcast_convert_fusion.6
  (75 shorter events, 16.8 us)
Async XLA Ops:
  6.5 42.1 %copy-start = (s32[16,2]{0,1:T(2,128)S(1)}, s32[16,2]{0,1:T(2,128)}, u32[]{:S(2)}) copy-start(s32[16,2]{0,1:T(2,128)} %param.11) | copy-start | bytes 388
  6.5 77.8 %all-gather.3.cloned.1.call-start = ((), (), s32[]{:S(2)}) async-start(), calls=%async_computation.1 | async-start | bytes 6144000 | tf_op jit(solution)/shard_map/all_gather | solution.py:62
  46.7 0.7 copy-start.1
Sparse Core Ops, SparseCore 0:
  46.9 37.4 all-gather.2
where the time goes:
time: 144 us; the launch traced here: 143 us
  blocking collectives  36.9 us (26%)
  waiting for transfers between devices  35.6 us (25%)
  other arithmetic  18.1 us (13%)
  matrix products  15.4 us (11%)
  loops' own time  15.3 us (11%)
  between operations  14.1 us (10%)
  local copies, waits for them, and re-layouts  7.39 us (5%)
    all_to_all x1, blocking collectives, on_device(): lax.all_to_all(complex_images, 'tile', split_axis=2, concat_axis=1, tiled...  36.9 us
    all_gather x1, waiting for transfers between devices, on_device(): gathered = lax.all_gather(stack, 'date', axis=0, tiled=True)  35.6 us
    dot_general x16, matrix products, looks(): jnp.dot(values, box, precision=lax.Precision.HIGHEST, preferred_element_t...  15.4 us
    another operation x1, loops' own time, tile_looks(): return lax.map(one_pair, jnp.stack([first_idx, second_idx], axis=1))  15 us
    convert_element_type x8, other arithmetic, date_power(): image = image.astype(jnp.float32)  9.26 us
    convert_element_type x4, other arithmetic, one_pair(): lax.dynamic_index_in_dim(stack, indices[0], 0, keepdims=False)  5.7 us
  transfers between devices with their start and end apart: 1, of which 1 were waited for; matrix products, arithmetic and copies ran while one was open for 1% of the time, Pallas kernels for 0%

commit v1 on v0

v1 whole, which is shorter than its diff:
```python
import functools

import jax
import jax.numpy as jnp
from jax import lax
from jax.experimental import pallas as pl
from jax.experimental.pallas import tpu as pltpu
from jax.sharding import PartitionSpec as P

LOOK_RG = 15
LOOK_AZ = 5
LANES = 128
EPS = 1e-05


def remote(src, dst, send_sem, recv_sem, tile, date):
    return pltpu.make_async_remote_copy(
        src_ref=src,
        dst_ref=dst,
        send_sem=send_sem,
        recv_sem=recv_sem,
        device_id={"tile": tile, "date": date},
        device_id_type=pl.DeviceIdType.MESH,
    )


def kernel(
    nt, nd, x_ref, pos_ref, usable_ref, ep_ref, out_ref,
    raw, plain, swapped, box, sums, looked, res, gath, rank_ref,
    send_sem, recv_sem, own_sem, res_send, res_recv, res_own,
):
    dates, tl, lines, padded, _, _ = raw.shape
    dl = dates // nd
    chunks = x_ref.shape[4]
    rows = 2 * padded
    pairs = ep_ref.shape[1]
    kl = pairs // nd
    looks = lines // LOOK_AZ
    i = lax.axis_index("tile")
    g = lax.axis_index("date")
    home = i // tl

    barrier = pltpu.get_barrier_semaphore()
    for s in range(1, nd):
        pl.semaphore_signal(
            barrier, inc=1, device_id={"tile": i, "date": lax.rem(g + s, nd)},
            device_id_type=pl.DeviceIdType.MESH,
        )

    def greet(b, carry):
        @pl.when(jnp.logical_or(b != i, home != g))
        def _():
            pl.semaphore_signal(
                barrier, inc=1, device_id={"tile": b, "date": home},
                device_id_type=pl.DeviceIdType.MESH,
            )
        return carry

    lax.fori_loop(0, nt, greet, 0)

    def own_copy(j):
        return pltpu.make_async_copy(
            x_ref.at[:, 0, g * tl + j], raw.at[pl.ds(g * dl, dl), j, :, pl.ds(0, chunks)],
            own_sem.at[j],
        )

    def raw_send(j, s):
        h = lax.rem(g + s, nd)
        return remote(
            x_ref.at[:, 0, h * tl + j], raw.at[pl.ds(g * dl, dl), j, :, pl.ds(0, chunks)],
            send_sem.at[j, s - 1], recv_sem.at[j, s - 1], i, h,
        )

    def raw_recv(j, s):
        h = lax.rem(g + nd - s, nd)
        return remote(
            x_ref.at[:, 0, j], raw.at[pl.ds(h * dl, dl), j, :, pl.ds(0, chunks)],
            send_sem.at[j, s - 1], recv_sem.at[j, s - 1], i, h,
        )

    for j in range(tl):
        own_copy(j).start()
    pl.semaphore_wait(barrier, nd - 1 + nd * tl - jnp.where(home == g, 1, 0))
    for j in range(tl):
        for s in range(1, nd):
            raw_send(j, s).start()

    col = lax.broadcasted_iota(jnp.int32, (LANES, LANES), 1) * LOOK_RG
    row = lax.broadcasted_iota(jnp.int32, (LANES, LANES), 0)
    for c in range(chunks):
        off = row + c * LANES - col
        box[c] = jnp.where(
            jnp.logical_and(off >= 0, off < LOOK_RG), 1.0, 0.0
        ).astype(jnp.bfloat16)

    def rank_of(p, carry):
        rank_ref[p] = lax.fori_loop(
            0, nt, lambda b, r: jnp.where(pos_ref[0, b] == p, b, r), 0
        )
        return carry

    lax.fori_loop(0, nt, rank_of, 0)

    view = raw.reshape(dates, tl, lines, rows, LANES)
    even = lax.broadcasted_iota(jnp.int32, (rows // 8, 8, LANES), 1) % 2 == 0
    items = 2 * pairs + dates

    def unpack(j, d):
        for a in range(looks):
            total = None
            for l in range(a * LOOK_AZ, (a + 1) * LOOK_AZ):
                v = view[d, j, l].astype(jnp.float32)
                plain[d, l] = v
                v8 = v.reshape(rows // 8, 8, LANES)
                swapped[d, l] = jnp.where(
                    even, -pltpu.roll(v8, 7, 1), pltpu.roll(v8, 1, 1)
                ).reshape(rows, LANES)
                total = v * v if total is None else total + v * v
            sums[pl.ds(((2 * pairs + d) * looks + a) * rows, rows)] = total

    def pair(k, carry):
        fa = ep_ref[0, k]
        fb = ep_ref[1, k]
        for a in range(looks):
            re = im = None
            for l in range(a * LOOK_AZ, (a + 1) * LOOK_AZ):
                va = plain[fa, l]
                tr = va * plain[fb, l]
                ti = va * swapped[fb, l]
                re = tr if re is None else re + tr
                im = ti if im is None else im + ti
            sums[pl.ds(pl.multiple_of(((2 * k) * looks + a) * rows, 8), rows)] = re
            sums[pl.ds(pl.multiple_of(((2 * k + 1) * looks + a) * rows, 8), rows)] = im
        return carry

    for j in range(tl):
        own_copy(j).wait()
        for s in range(1, nd):
            raw_recv(j, s).wait_recv()

        def unpack_step(d, carry):
            unpack(j, d)
            return carry

        lax.fori_loop(0, dates, unpack_step, 0)
        lax.fori_loop(0, pairs, pair, 0)
        n = items * looks
        acc = jnp.zeros((n, LANES), jnp.float32)
        for c in range(chunks):
            v = sums[pl.ds(2 * c, n, stride=rows)] + sums[pl.ds(2 * c + 1, n, stride=rows)]
            hi = v.astype(jnp.bfloat16)
            left = v - hi.astype(jnp.float32)
            mid = left.astype(jnp.bfloat16)
            low = (left - mid.astype(jnp.float32)).astype(jnp.bfloat16)
            for part in (hi, mid, low):
                acc = acc + jnp.dot(part, box[c], preferred_element_type=jnp.float32)
        acc = acc * (1.0 / (LOOK_AZ * LOOK_RG))
        for it in range(items):
            part = acc[it * looks:(it + 1) * looks]
            looked[it] = part if it < 2 * pairs else lax.rsqrt(part + EPS)
        for k in range(pairs):
            w = looked[2 * pairs + ep_ref[0, k]] * looked[2 * pairs + ep_ref[1, k]]
            res[j, k, 0] = looked[2 * k] * w
            res[j, k, 1] = looked[2 * k + 1] * w
        for h in range(nd):
            t = g * tl + j
            mine = jnp.logical_and(t == i, h == g)

            @pl.when(mine)
            def _():
                pltpu.make_async_copy(
                    res.at[j, pl.ds(h * kl, kl)], gath.at[i], res_own
                ).start()

            @pl.when(jnp.logical_not(mine))
            def _():
                remote(
                    res.at[j, pl.ds(h * kl, kl)], gath.at[i],
                    res_send.at[j, h], res_recv.at[i], t, h,
                ).start()

    def land(b, carry):
        here = jnp.logical_and(b == i, home == g)

        @pl.when(here)
        def _():
            pltpu.make_async_copy(res.at[0, pl.ds(0, kl)], gath.at[b], res_own).wait()

        @pl.when(jnp.logical_not(here))
        def _():
            remote(
                res.at[0, pl.ds(0, kl)], gath.at[b],
                res_send.at[0, 0], res_recv.at[b], i, g,
            ).wait_recv()
        return carry

    lax.fori_loop(0, nt, land, 0)
    for p in range(nt):
        valid = jnp.where(p < usable_ref[0], 1.0, 0.0).astype(jnp.float32)
        out_ref[:, :, p * looks:(p + 1) * looks, :] = gath[rank_ref[p]] * valid

    for j in range(tl):
        for s in range(1, nd):
            raw_send(j, s).wait_send()
        for h in range(nd):
            mine = jnp.logical_and(g * tl + j == i, h == g)

            @pl.when(jnp.logical_not(mine))
            def _():
                remote(
                    res.at[j, pl.ds(h * kl, kl)], gath.at[i],
                    res_send.at[j, h], res_recv.at[i], g * tl + j, h,
                ).wait_send()


def on_device(nt, nd, complex_images, segment_position_map, usable_position_total, interferogram_epochs):
    dl, bl, tiles, _, lines, width = complex_images.shape
    assert bl == 1 and tiles == nt
    chunks = width // LANES
    padded = -(-chunks // 8) * 8
    x = complex_images.reshape(dl, bl, tiles, 2, lines, chunks, LANES)
    x = x.transpose(0, 1, 2, 4, 5, 3, 6)
    dates = dl * nd
    tl = tiles // nd
    pairs = interferogram_epochs.shape[0]
    kl = pairs // nd
    looks = lines // LOOK_AZ
    items = 2 * pairs + dates
    dma = pltpu.SemaphoreType.DMA
    f32 = jnp.float32
    smem = pl.BlockSpec(memory_space=pltpu.SMEM)
    return pl.pallas_call(
        functools.partial(kernel, nt, nd),
        out_shape=jax.ShapeDtypeStruct((kl, 2, nt * looks, width // LOOK_RG), f32),
        in_specs=[pl.BlockSpec(memory_space=pltpu.HBM), smem, smem, smem],
        out_specs=pl.BlockSpec(memory_space=pltpu.VMEM),
        scratch_shapes=[
            pltpu.VMEM((dates, tl, lines, padded, 2, LANES), jnp.bfloat16),
            pltpu.VMEM((dates, lines, 2 * padded, LANES), f32),
            pltpu.VMEM((dates, lines, 2 * padded, LANES), f32),
            pltpu.VMEM((chunks, LANES, LANES), jnp.bfloat16),
            pltpu.VMEM((items * looks * 2 * padded, LANES), f32),
            pltpu.VMEM((items, looks, LANES), f32),
            pltpu.VMEM((tl, pairs, 2, looks, LANES), f32),
            pltpu.VMEM((nt, kl, 2, looks, LANES), f32),
            pltpu.SMEM((nt,), jnp.int32),
            dma((tl, nd - 1)),
            dma((tl, nd - 1)),
            dma((tl,)),
            dma((tl, nd)),
            dma((nt,)),
            dma,
        ],
        compiler_params=pltpu.CompilerParams(
            collective_id=0, has_side_effects=True, vmem_limit_bytes=48 * 1024 * 1024
        ),
        name="coherence",
    )(x, segment_position_map, usable_position_total, interferogram_epochs.T)


def solution(mesh):
    in_specs = (P("date", "tile", None, None, None, None), P("tile", None), P("tile"), P())
    out_specs = P("date", None, None, "tile")
    body = functools.partial(on_device, mesh.shape["tile"], mesh.shape["date"])
    return jax.shard_map(
        body, mesh=mesh, in_specs=in_specs, out_specs=out_specs, check_vma=False
    )
```

time: 144 us -> 29.2 us (0.20)
  the two profiles are of different devices: /device:TPU:0 before, /device:TPU:15 now
where the time goes in v1:
time: 29.2 us; the launch traced here: 29 us
  Pallas kernels  25.1 us (86%)
  local copies, waits for them, and re-layouts  3.25 us (11%)
  between operations  0.67 us (2%)
    pallas_call x1, Pallas kernels, on_device(): pl.pallas_call(functools.partial(kernel, nt, nd), out_shape=jax.ShapeDtyp...  25.1 us
    unnamed x7, local copies, waits for them, and re-layouts  3.25 us

profile of v1, /device:TPU:15, one launch (start us, length us, event | category | flops | bytes accessed | tf_op | source)
XLA Modules:
  0.0 29.0 jit_solution(8219232866341729909)
XLA Ops:
  0.7 0.0 copy-start
  0.7 1.3 %copy-done = bf16[2,1,8,2,10,1920]{5,3,4,2,1,0:T(2,128)(2,1)S(1)} copy-done((bf16[2,1,8,2,10,1920]{5,3,4,2,1,0:T(2,128)(2,1)S(1)}, bf16[2,1,8,2,10,1920]{5,3,4,2,1,0:T(2,128)(2,1)}, u32[]{:S(2)}) %copy-start) | copy-done | bytes 1228824
  1.9 0.0 copy-start.1
  1.9 0.7 %copy-done.1 = s32[16,2]{0,1:T(2,128)S(1)} copy-done((s32[16,2]{0,1:T(2,128)S(1)}, s32[16,2]{0,1:T(2,128)}, u32[]{:S(2)}) %copy-start.1) | copy-done | bytes 152
  2.6 0.0 copy-start.2
  2.6 0.7 %copy-done.2 = s32[1,8]{1,0:T(1,128)S(1)} copy-done((s32[1,8]{1,0:T(1,128)S(1)}, s32[1,8]{1,0:T(1,128)}, u32[]{:S(2)}) %copy-start.2) | copy-done | bytes 56
  3.3 25.1 %coherence.1 = f32[4,2,16,128]{3,2,1,0:T(8,128)S(1)} custom-call(bf16[2,1,8,10,15,2,128]{6,5,4,3,2,1,0:T(2,128)(2,1)S(1)} %bitcast.4, s32[1,8]{1,0:T(1,128)S(1)} %copy-done.2, s32[1]{0:T(128)S(6)} %copy.6.usable_ref, s32[2,16]{1,0:T(2,128)S(1)} %bitcast.5), custom_call_target="tpu_custom_call" | custom-call | tf_op jit(solution)/shard_map/coherence/pallas_call | solution.py:232
  28.4 0.6 %copy.7 = f32[4,2,16,128]{3,2,1,0:T(8,128)} copy(f32[4,2,16,128]{3,2,1,0:T(8,128)S(1)} %coherence.1) | data formatting | bytes 131072
Async XLA Ops:
  0.7 1.3 %copy-start = (bf16[2,1,8,2,10,1920]{5,3,4,2,1,0:T(2,128)(2,1)S(1)}, bf16[2,1,8,2,10,1920]{5,3,4,2,1,0:T(2,128)(2,1)}, u32[]{:S(2)}) copy-start(bf16[2,1,8,2,10,1920]{5,3,4,2,1,0:T(2,128)(2,1)} %param.4) | copy-start | bytes 3686404
  1.9 0.7 %copy-start.1 = (s32[16,2]{0,1:T(2,128)S(1)}, s32[16,2]{0,1:T(2,128)}, u32[]{:S(2)}) copy-start(s32[16,2]{0,1:T(2,128)} %param.7) | copy-start | bytes 388
  2.6 0.7 %copy-start.2 = (s32[1,8]{1,0:T(1,128)S(1)}, s32[1,8]{1,0:T(1,128)}, u32[]{:S(2)}) copy-start(s32[1,8]{1,0:T(1,128)} %pos_ref.1) | copy-start | bytes 100

commit v2 on v1

v2 whole, which is shorter than its diff:
```python
import functools

import jax
import jax.numpy as jnp
from jax import lax
from jax.experimental import pallas as pl
from jax.experimental.pallas import tpu as pltpu
from jax.sharding import PartitionSpec as P

LOOK_RG = 15
LOOK_AZ = 5
LANES = 128
EPS = 1e-05


def remote(src, dst, send_sem, recv_sem, tile, date):
    return pltpu.make_async_remote_copy(
        src_ref=src,
        dst_ref=dst,
        send_sem=send_sem,
        recv_sem=recv_sem,
        device_id={"tile": tile, "date": date},
        device_id_type=pl.DeviceIdType.MESH,
    )


def bitwise_xor(a, b, bits):
    total = 0
    for s in range(bits):
        total = total + lax.rem(a // 2**s + b // 2**s, 2) * 2**s
    return total


def kernel(
    nt, nd, x_ref, pos_ref, usable_ref, ep_ref, out_ref,
    raw, plain, swapped, box, sums, looked, res, gath, rank_ref,
    send_sem, recv_sem, own_sem, res_send, res_recv, res_own, round_sem,
):
    dates, tl, lines, padded, _, _ = raw.shape
    dl = dates // nd
    chunks = x_ref.shape[4]
    rows = 2 * padded
    pairs = ep_ref.shape[1]
    kl = pairs // nd
    looks = lines // LOOK_AZ
    items = 2 * pairs + dates
    bits = nt.bit_length() - 1
    i = lax.axis_index("tile")
    g = lax.axis_index("date")

    def tile_of(j, h):
        return bitwise_xor(i, (tl - 1 - j) * nd + h, bits)

    def signal(sem, tile, date):
        pl.semaphore_signal(
            sem, inc=1, device_id={"tile": tile, "date": date},
            device_id_type=pl.DeviceIdType.MESH,
        )

    barrier = pltpu.get_barrier_semaphore()
    for r in range(bits):
        signal(barrier, bitwise_xor(i, 2**r, bits), g)
    for s in range(1, nd):
        signal(barrier, i, lax.rem(g + s, nd))

    def slot(date, j, a):
        return raw.at[
            pl.ds(date * dl, dl), j, pl.ds(a * LOOK_AZ, LOOK_AZ), pl.ds(0, chunks)
        ]

    def source(tile, a):
        return x_ref.at[:, 0, tile, pl.ds(a * LOOK_AZ, LOOK_AZ)]

    def own_copy(j, a):
        return pltpu.make_async_copy(source(tile_of(j, g), a), slot(g, j, a), own_sem.at[j, a])

    def raw_send(j, a, s):
        h = lax.rem(g + s, nd)
        return remote(
            source(tile_of(j, h), a), slot(g, j, a),
            send_sem.at[j, a, s - 1], recv_sem.at[j, a, s - 1], i, h,
        )

    def raw_recv(j, a, s):
        h = lax.rem(g + nd - s, nd)
        return remote(
            source(i, a), slot(h, j, a),
            send_sem.at[j, a, s - 1], recv_sem.at[j, a, s - 1], i, h,
        )

    parts = [(j, a) for j in range(tl) for a in range(looks)]
    for j, a in parts:
        own_copy(j, a).start()
    pl.semaphore_wait(barrier, nd - 1 + bits)
    for j, a in parts:
        for s in range(1, nd):
            raw_send(j, a, s).start()

    for r in range(bits):
        signal(round_sem.at[r], bitwise_xor(i, 2**r, bits), g)
        pl.semaphore_wait(round_sem.at[r], 1)

    col = lax.broadcasted_iota(jnp.int32, (LANES, LANES), 1) * LOOK_RG
    row = lax.broadcasted_iota(jnp.int32, (LANES, LANES), 0)
    for c in range(chunks):
        off = row + c * LANES - col
        box[pl.ds(c * LANES, LANES)] = jnp.where(
            jnp.logical_and(off >= 0, off < LOOK_RG), 1.0, 0.0
        ).astype(jnp.bfloat16)

    def rank_of(p, carry):
        rank_ref[p] = lax.fori_loop(
            0, nt, lambda b, r: jnp.where(pos_ref[0, b] == p, b, r), 0
        )
        return carry

    lax.fori_loop(0, nt, rank_of, 0)

    view = raw.reshape(dates, tl, lines, rows, LANES)
    even = lax.broadcasted_iota(jnp.int32, (rows // 8, 8, LANES), 1) % 2 == 0

    def unpack(j, a, d):
        total = None
        for l in range(LOOK_AZ):
            v = view[d, j, a * LOOK_AZ + l].astype(jnp.float32)
            plain[d, l] = v
            v8 = v.reshape(rows // 8, 8, LANES)
            swapped[d, l] = jnp.where(
                even, -pltpu.roll(v8, 7, 1), pltpu.roll(v8, 1, 1)
            ).reshape(rows, LANES)
            total = v * v if total is None else total + v * v
        sums[pl.ds(pl.multiple_of((2 * pairs + d) * rows, 8), rows)] = total

    def pair(k, carry):
        fa = ep_ref[0, k]
        fb = ep_ref[1, k]
        re = im = None
        for l in range(LOOK_AZ):
            va = plain[fa, l]
            tr = va * plain[fb, l]
            ti = va * swapped[fb, l]
            re = tr if re is None else re + tr
            im = ti if im is None else im + ti
        sums[pl.ds(pl.multiple_of(k * rows, 8), rows)] = re
        sums[pl.ds(pl.multiple_of((pairs + k) * rows, 8), rows)] = im
        return carry

    for j, a in parts:
        for s in range(nd):
            if s == 0:
                own_copy(j, a).wait()
            else:
                raw_recv(j, a, s).wait_recv()
            h = lax.rem(g + nd - s, nd)
            for d in range(dl):
                unpack(j, a, h * dl + d)
        lax.fori_loop(0, pairs, pair, 0)
        hi, low = [], []
        for c in range(chunks):
            v = (
                sums[pl.ds(2 * c, items, stride=rows)]
                + sums[pl.ds(2 * c + 1, items, stride=rows)]
            )
            top = v.astype(jnp.bfloat16)
            hi.append(top)
            low.append((v - top.astype(jnp.float32)).astype(jnp.bfloat16))
        weights = box[...]
        acc = jnp.dot(
            jnp.concatenate(hi, axis=1), weights, preferred_element_type=jnp.float32
        ) + jnp.dot(jnp.concatenate(low, axis=1), weights, preferred_element_type=jnp.float32)
        acc = acc * (1.0 / (LOOK_AZ * LOOK_RG))
        looked[pl.ds(0, 2 * pairs)] = acc[:2 * pairs]
        looked[pl.ds(2 * pairs, dates)] = lax.rsqrt(acc[2 * pairs:] + EPS)
        for k in range(pairs):
            w = (
                looked[pl.ds(2 * pairs + ep_ref[0, k], 1)]
                * looked[pl.ds(2 * pairs + ep_ref[1, k], 1)]
            )
            res[j, k, 0, a:a + 1] = looked[k:k + 1] * w
            res[j, k, 1, a:a + 1] = looked[pairs + k:pairs + k + 1] * w
        if a < looks - 1:
            continue
        t = tile_of(j, g)
        for h in range(nd):
            mine = jnp.logical_and(t == i, g == h)

            @pl.when(mine)
            def _():
                pltpu.make_async_copy(
                    res.at[j, pl.ds(h * kl, kl)], gath.at[i], res_own
                ).start()

            @pl.when(jnp.logical_not(mine))
            def _():
                remote(
                    res.at[j, pl.ds(h * kl, kl)], gath.at[i],
                    res_send.at[j, h], res_recv.at[i], t, h,
                ).start()

    def land(b, carry):
        here = jnp.logical_and(b == i, g == 0)

        @pl.when(here)
        def _():
            pltpu.make_async_copy(res.at[0, pl.ds(0, kl)], gath.at[b], res_own).wait()

        @pl.when(jnp.logical_not(here))
        def _():
            remote(
                res.at[0, pl.ds(0, kl)], gath.at[b],
                res_send.at[0, 0], res_recv.at[b], i, g,
            ).wait_recv()
        return carry

    lax.fori_loop(0, nt, land, 0)
    for p in range(nt):
        valid = jnp.where(p < usable_ref[0], 1.0, 0.0).astype(jnp.float32)
        out_ref[:, :, p * looks:(p + 1) * looks, :] = gath[rank_ref[p]] * valid

    for j, a in parts:
        for s in range(1, nd):
            raw_send(j, a, s).wait_send()
    for j in range(tl):
        for h in range(nd):
            t = tile_of(j, g)

            @pl.when(jnp.logical_not(jnp.logical_and(t == i, g == h)))
            def _():
                remote(
                    res.at[j, pl.ds(h * kl, kl)], gath.at[i],
                    res_send.at[j, h], res_recv.at[i], t, h,
                ).wait_send()


def on_device(nt, nd, complex_images, segment_position_map, usable_position_total, interferogram_epochs):
    dl, bl, tiles, _, lines, width = complex_images.shape
    assert bl == 1 and tiles == nt and nt & (nt - 1) == 0 and nt % nd == 0
    chunks = width // LANES
    padded = -(-chunks // 8) * 8
    x = complex_images.reshape(dl, bl, tiles, 2, lines, chunks, LANES)
    x = x.transpose(0, 1, 2, 4, 5, 3, 6)
    dates = dl * nd
    tl = tiles // nd
    pairs = interferogram_epochs.shape[0]
    kl = pairs // nd
    looks = lines // LOOK_AZ
    items = 2 * pairs + dates
    dma = pltpu.SemaphoreType.DMA
    f32 = jnp.float32
    smem = pl.BlockSpec(memory_space=pltpu.SMEM)
    return pl.pallas_call(
        functools.partial(kernel, nt, nd),
        out_shape=jax.ShapeDtypeStruct((kl, 2, nt * looks, width // LOOK_RG), f32),
        in_specs=[pl.BlockSpec(memory_space=pltpu.HBM), smem, smem, smem],
        out_specs=pl.BlockSpec(memory_space=pltpu.VMEM),
        scratch_shapes=[
            pltpu.VMEM((dates, tl, lines, padded, 2, LANES), jnp.bfloat16),
            pltpu.VMEM((dates, LOOK_AZ, 2 * padded, LANES), f32),
            pltpu.VMEM((dates, LOOK_AZ, 2 * padded, LANES), f32),
            pltpu.VMEM((chunks * LANES, width // LOOK_RG), jnp.bfloat16),
            pltpu.VMEM((items * 2 * padded, LANES), f32),
            pltpu.VMEM((items, LANES), f32),
            pltpu.VMEM((tl, pairs, 2, looks, LANES), f32),
            pltpu.VMEM((nt, kl, 2, looks, LANES), f32),
            pltpu.SMEM((nt,), jnp.int32),
            dma((tl, looks, nd - 1)),
            dma((tl, looks, nd - 1)),
            dma((tl, looks)),
            dma((tl, nd)),
            dma((nt,)),
            dma,
            pltpu.SemaphoreType.REGULAR((nt.bit_length() - 1,)),
        ],
        compiler_params=pltpu.CompilerParams(
            collective_id=0, has_side_effects=True
        ),
        name="coherence",
    )(x, segment_position_map, usable_position_total, interferogram_epochs.T)


def solution(mesh):
    in_specs = (P("date", "tile", None, None, None, None), P("tile", None), P("tile"), P())
    out_specs = P("date", None, None, "tile")
    body = functools.partial(on_device, mesh.shape["tile"], mesh.shape["date"])
    return jax.shard_map(
        body, mesh=mesh, in_specs=in_specs, out_specs=out_specs, check_vma=False
    )
```

time: 29.2 us -> 28.2 us (0.966)
  the two profiles are of different devices: /device:TPU:15 before, /device:TPU:0 now
where the time goes in v2:
time: 28.2 us; the launch traced here: 28 us
  Pallas kernels  25.9 us (92%)
  local copies, waits for them, and re-layouts  1.47 us (5%)
  between operations  0.66 us (2%)
    pallas_call x1, Pallas kernels, on_device(): pl.pallas_call(functools.partial(kernel, nt, nd), out_shape=jax.ShapeDtyp...  25.9 us
    unnamed x1, local copies, waits for them, and re-layouts  1.47 us

profile of v2, /device:TPU:0, one launch (start us, length us, event | category | flops | bytes accessed | tf_op | source)
XLA Modules:
  0.0 28.0 jit_solution(6279393835372525460)
XLA Ops:
  0.7 25.9 %coherence.1 = f32[4,2,16,128]{3,2,1,0:T(8,128)} custom-call(bf16[2,1,8,10,15,2,128]{6,5,4,3,2,1,0:T(2,128)(2,1)} %bitcast.4, s32[1,8]{1,0:T(1,128)} %pos_ref.1, s32[1]{0:T(128)S(6)} %copy.6.usable_ref, s32[2,16]{1,0:T(2,128)} %bitcast.5), custom_call_target="tpu_custom_call" | custom-call | tf_op jit(solution)/shard_map/coherence/pallas_call | solution.py:251
  26.5 1.5 %copy.7 = f32[4,2,16,128]{3,2,1,0:T(8,128)} copy(f32[4,2,16,128]{3,2,1,0:T(8,128)} %coherence.1) | data formatting | bytes 131072

commit v3 on v2

--- a/solution.py
+++ b/solution.py
@@ -32,15 +32,15 @@
 
 
 def kernel(
-    nt, nd, x_ref, pos_ref, usable_ref, ep_ref, out_ref,
-    raw, plain, swapped, box, sums, looked, res, gath, rank_ref,
+    nt, nd, x_ref, pos_hbm, usable_hbm, ep_hbm, out_ref,
+    pos_ref, usable_ref, ep_ref, small_sem, raw, plain, swapped, box, sums, looked, res, gath, rank_ref,
     send_sem, recv_sem, own_sem, res_send, res_recv, res_own, round_sem,
 ):
     dates, tl, lines, padded, _, _ = raw.shape
     dl = dates // nd
     chunks = x_ref.shape[4]
     rows = 2 * padded
-    pairs = ep_ref.shape[1]
+    pairs = ep_hbm.shape[1]
     kl = pairs // nd
     looks = lines // LOOK_AZ
     items = 2 * pairs + dates
@@ -58,10 +58,14 @@
         )
 
     barrier = pltpu.get_barrier_semaphore()
-    for r in range(bits):
-        signal(barrier, bitwise_xor(i, 2**r, bits), g)
     for s in range(1, nd):
         signal(barrier, i, lax.rem(g + s, nd))
+    side = i + 1 - 2 * lax.rem(i, 2)
+    signal(barrier, side, g)
+    below = i >= 2
+    above = i < nt - 2
+    pl.when(below)(lambda: signal(barrier, i - 2, g))
+    pl.when(above)(lambda: signal(barrier, i + 2, g))
 
     def slot(date, j, a):
         return raw.at[
@@ -91,14 +95,31 @@
     parts = [(j, a) for j in range(tl) for a in range(looks)]
     for j, a in parts:
         own_copy(j, a).start()
-    pl.semaphore_wait(barrier, nd - 1 + bits)
+    pl.semaphore_wait(
+        barrier, nd + jnp.where(below, 1, 0) + jnp.where(above, 1, 0)
+    )
     for j, a in parts:
         for s in range(1, nd):
             raw_send(j, a, s).start()
 
-    for r in range(bits):
-        signal(round_sem.at[r], bitwise_xor(i, 2**r, bits), g)
-        pl.semaphore_wait(round_sem.at[r], 1)
+    small = [
+        pltpu.make_async_copy(src, dst, small_sem.at[n])
+        for n, (src, dst) in enumerate(
+            ((pos_hbm, pos_ref), (usable_hbm, usable_ref), (ep_hbm, ep_ref))
+        )
+    ]
+    for copy in small:
+        copy.start()
+
+    signal(round_sem.at[0], side, g)
+    pl.semaphore_wait(round_sem.at[0], 1)
+    for step, ahead, behind in ((2, above, below), (-2, below, above)):
+        sem = round_sem.at[1 if step > 0 else 2]
+        pl.when(behind)(functools.partial(pl.semaphore_wait, sem, 1))
+        pl.when(ahead)(functools.partial(signal, sem, i + step, g))
+
+    for copy in small:
+        copy.wait()
 
     col = lax.broadcasted_iota(jnp.int32, (LANES, LANES), 1) * LOOK_RG
     row = lax.broadcasted_iota(jnp.int32, (LANES, LANES), 0)
@@ -247,13 +268,16 @@
     items = 2 * pairs + dates
     dma = pltpu.SemaphoreType.DMA
     f32 = jnp.float32
-    smem = pl.BlockSpec(memory_space=pltpu.SMEM)
     return pl.pallas_call(
         functools.partial(kernel, nt, nd),
         out_shape=jax.ShapeDtypeStruct((kl, 2, nt * looks, width // LOOK_RG), f32),
-        in_specs=[pl.BlockSpec(memory_space=pltpu.HBM), smem, smem, smem],
+        in_specs=[pl.BlockSpec(memory_space=pltpu.HBM)] * 4,
         out_specs=pl.BlockSpec(memory_space=pltpu.VMEM),
         scratch_shapes=[
+            pltpu.SMEM((1, nt), jnp.int32),
+            pltpu.SMEM((1,), jnp.int32),
+            pltpu.SMEM((2, pairs), jnp.int32),
+            dma((3,)),
             pltpu.VMEM((dates, tl, lines, padded, 2, LANES), jnp.bfloat16),
             pltpu.VMEM((dates, LOOK_AZ, 2 * padded, LANES), f32),
             pltpu.VMEM((dates, LOOK_AZ, 2 * padded, LANES), f32),
@@ -269,7 +293,7 @@
             dma((tl, nd)),
             dma((nt,)),
             dma,
-            pltpu.SemaphoreType.REGULAR((nt.bit_length() - 1,)),
+            pltpu.SemaphoreType.REGULAR((3,)),
         ],
         compiler_params=pltpu.CompilerParams(
             collective_id=0, has_side_effects=True

time: 28.2 us -> 27 us (0.957)
  Pallas kernels: 25.9 us -> 24.7 us
    pallas_call x1, Pallas kernels: 25.9 us -> 24.7 us  [on_device(): pl.pallas_call(functools.partial(kernel, nt, nd), out_shape=jax.ShapeDtyp...]
where the time goes in v3:
time: 27 us; the launch traced here: 26.8 us
  Pallas kernels  24.7 us (91%)
  local copies, waits for them, and re-layouts  1.47 us (5%)
  between operations  0.66 us (2%)
    pallas_call x1, Pallas kernels, on_device(): pl.pallas_call(functools.partial(kernel, nt, nd), out_shape=jax.ShapeDtyp...  24.7 us
    unnamed x1, local copies, waits for them, and re-layouts  1.47 us

profile of v3, /device:TPU:0, one launch (start us, length us, event | category | flops | bytes accessed | tf_op | source)
XLA Modules:
  0.0 26.8 jit_solution(12670621422240372106)
XLA Ops:
  0.7 24.7 %coherence.1 = f32[4,2,16,128]{3,2,1,0:T(8,128)} custom-call(bf16[2,1,8,10,15,2,128]{6,5,4,3,2,1,0:T(2,128)(2,1)} %bitcast.4, s32[1,8]{1,0:T(1,128)} %pos_hbm.1, s32[1]{0:T(128)S(6)} %copy.6.usable_hbm, s32[2,16]{1,0:T(2,128)} %bitcast.5), custom_call_target="tpu_custom_call" | custom-call | tf_op jit(solution)/shard_map/coherence/pallas_call | solution.py:271
  25.4 1.5 %copy.7 = f32[4,2,16,128]{3,2,1,0:T(8,128)} copy(f32[4,2,16,128]{3,2,1,0:T(8,128)} %coherence.1) | data formatting | bytes 131072
